TPU v7x, 32 devices: a whole 2x2x4 slice. The times are simulated.
32 devices in a mesh: lat: 4 (over z), lon: 8 (over y, x, core).
Axes of the slice: x: 2, y: 2, z: 4, core: 2. Of those that a mesh axis runs over, the one named last changes fastest.
Arguments:
- samples: bfloat16 [256, 90112], P(None, ('lat', 'lon')), may hold values from -6 to 6
- area_weight: float32 [90112], P(('lat', 'lon')), may hold values from 0.1 to 1
- ocean_count: int32 [4, 8], P('lat', 'lon'), may hold values from 704 to 2816, as said below
- omega: bfloat16 [512, 256], replicated, may hold values from -5 to 5
Outputs:
- point_basis: bfloat16 [512, 90112], P(None, ('lat', 'lon'))
- sample_basis: float32 [8, 256, 64], replicated
Inputs may be any that keep to these rules, and one draw needn't show every extreme that they name: Each device's block of grid points starts with ocean_count ocean points, the rest are land; some device's block is all ocean (2816).
All inputs are finite; a program needn't handle non-finite values.
Results may differ from a plain program's by a relative error of at most 0.0075.
Values sent between devices are 32-bit elements; how exact they have to be, the bound alone decides.
No kernel may reach another device: no remote copies, remote signals or barrier semaphores. Data moves between devices by JAX's collectives and lax.ppermute only.
A program may use at most 64 MiB of HBM per device.

v0:
```python
import jax
import jax.numpy as jnp
from jax import lax
from jax.sharding import PartitionSpec as P

SAMPLES = 256
COLUMNS = 64
FOLDS = 8


def grid_total(partial_value):
    return lax.psum(partial_value, ("lat", "lon"))


def on_device(samples, area_weight, ocean_count, omega):
    point_cols = samples.shape[1]
    fold_row = lax.iota(jnp.int32, FOLDS * COLUMNS) // COLUMNS
    fold_col = lax.iota(jnp.int32, SAMPLES) // (SAMPLES // FOLDS)
    keeping = fold_row[:, None] != fold_col[None, :]
    live = jnp.where(keeping, omega, jnp.zeros_like(omega))
    valid = lax.iota(jnp.int32, point_cols) < ocean_count[0, 0]
    weighted = jnp.where(
        valid[None, :], samples.astype(jnp.float32) * area_weight[None, :], jnp.float32(0.0)
    ).astype(jnp.bfloat16)
    product = jnp.dot(live, weighted, preferred_element_type=jnp.float32)
    scores = product.astype(jnp.bfloat16)
    folded = scores.reshape(FOLDS, COLUMNS, point_cols)
    devices_all = lax.axis_size("lat") * lax.axis_size("lon")
    total = point_cols * devices_all
    exact = product.reshape(FOLDS, COLUMNS, point_cols)
    partial_gram = jnp.einsum("fkp,fjp->fkj", exact, exact, precision=lax.Precision.HIGHEST)
    gram = grid_total(partial_gram)
    partial_cross = jnp.einsum(
        "sp,fkp->fsk", weighted.astype(jnp.float32), exact, precision=lax.Precision.HIGHEST
    )
    lower_factor = jnp.linalg.cholesky(gram)
    identity = jnp.broadcast_to(jnp.eye(COLUMNS, dtype=jnp.float32), (FOLDS, COLUMNS, COLUMNS))
    inverse = jax.scipy.linalg.solve_triangular(lower_factor, identity, lower=True)
    point_scale = (inverse * jnp.float32(total**0.5)).astype(jnp.bfloat16)
    point_basis = jnp.einsum(
        "fkj,fjp->fkp", point_scale, folded, preferred_element_type=jnp.float32
    )
    point_basis = point_basis.astype(jnp.bfloat16).reshape(FOLDS * COLUMNS, point_cols)
    sample_scale = inverse * jnp.float32((SAMPLES / total) ** 0.5)
    cross = lax.psum(partial_cross, ("lat", "lon"))
    sample_basis = jnp.einsum("fsj,fkj->fsk", cross, sample_scale, precision=lax.Precision.HIGHEST)
    return (point_basis, sample_basis)


def solution(mesh):
    in_specs = (P(None, ("lat", "lon")), P(("lat", "lon")), P("lat", "lon"), P())
    out_specs = (P(None, ("lat", "lon")), P())
    return jax.shard_map(
        on_device, mesh=mesh, in_specs=in_specs, out_specs=out_specs, check_vma=False
    )
```

profile of v0, /device:TPU:0, one launch (start us, length us, event | category | flops | bytes accessed | tf_op | source)
XLA Modules:
  0.0 253.4 jit_solution(10656014839347430208)
XLA Ops:
  7.2 0.0 all-reduce.3.cloned.1.call-start
  7.9 0.0 copy-start
  7.9 0.0 copy-start.1
  7.9 2.5 fusion.26
  10.4 0.0 copy-done
  10.4 0.0 copy-done.1
  10.4 3.7 %fusion.2 = f32[8,256,64]{1,2,0:T(8,128)} fusion(f32[8,64,2816]{2,1,0:T(8,128)S(1)} %bitcast.26, bf16[256,2816]{1,0:T(8,128)(2,1)S(1)} %copy-done, f32[2816]{0:T(1024)S(1)} %copy-done.1, pred[2816]{0:T(1024)(128)(4,1)S(1)} %iota_compare_fusion.2), kind=kOutput, calls=%fused_computation.4 | convolution fusion | flops 4432068608 | bytes 7747328 | tf_op jit(solution)/shard_map/sp,fkp->fsk/dot_general | solution.py:33
  14.1 5.9 %fusion.27 = f32[8,64,64]{1,2,0:T(8,128)} fusion(f32[8,64,2816]{2,1,0:T(8,128)S(1)} %bitcast.27), kind=kOutput, calls=%fused_computation.44 | convolution fusion | flops 1107296256 | bytes 5898240 | tf_op jit(solution)/shard_map/fkp,fjp->fkj/dot_general | solution.py:31
  20.0 0.0 all-reduce.3.cloned.1.call-update
  20.0 132.2 %all-reduce.3.cloned.1.call-done = (f32[8,64,64]{1,2,0:T(8,128)}, f32[8,256,64]{1,2,0:T(8,128)}) async-done(((f32[8,64,64]{1,2,0:T(8,128)}, f32[8,256,64]{1,2,0:T(8,128)}), (f32[8,64,64]{1,2,0:T(8,128)}, f32[8,256,64]{1,2,0:T(8,128)})) %all-reduce.3.cloned.1.call-update) | async-done | bytes 655376 | tf_op jit(solution)/shard_map/psum | solution.py:12
  152.3 1.1 copy.10
  153.4 1.0 fusion.8
  154.3 47.1 %custom-call.8 = f32[8,64,64]{2,1,0:T(8,128)S(1)} custom-call(f32[8,64,64]{2,1,0:T(8,128)S(1)} %fusion.8), custom_call_target="Cholesky" | custom-call | tf_op jit(solution)/shard_map/jit(cholesky)/cholesky | solution.py:36
  201.5 0.1 compare_reduce_fusion
  201.6 0.1 select_bitcast_fusion
  201.7 39.3 %custom-call.9 = f32[8,1,64,64]{2,3,1,0:T(8,128)S(1)} custom-call(f32[8,1,64,64]{3,2,1,0:T(8,128)S(1)} %select_bitcast_fusion), custom_call_target="InvertDiagBlocksLowerTriangular" | custom-call | tf_op jit(solution)/shard_map/jit(_solve_triangular)/vmap()/triangular_solve | solution.py:38
  241.0 0.6 fusion.6
  241.6 2.4 fusion.9
  244.1 2.5 convolution_convert_fusion
  (7 shorter events, 0.1 us)
Async XLA Ops:
  7.2 145.1 %all-reduce.3.cloned.1.call-start = ((), (), s32[]{:S(2)}) async-start(), calls=%async_computation | async-start | bytes 1572864 | tf_op jit(solution)/shard_map/psum | solution.py:12
  7.9 2.5 copy-start
  7.9 2.5 copy-start.1
Sparse Core Ops, SparseCore 0:
  20.1 132.1 all-reduce.2
where the time goes:
time: 254 us; the launch traced here: 253 us
  waiting for transfers between devices  132 us (52%)
  other arithmetic  87.7 us (35%)
  matrix products  17.5 us (7%)
  between operations  14.8 us (6%)
    psum x1, waiting for transfers between devices, grid_total(): return lax.psum(partial_value, ('lat', 'lon'))  132 us
    another operation x4, other arithmetic, on_device(): lower_factor = jnp.linalg.cholesky(gram)  47.2 us
    another operation x3, other arithmetic, on_device(): jax.scipy.linalg.solve_triangular(lower_factor, identity, lower=True)  39.4 us
    dot_general x1, matrix products, on_device(): jnp.einsum('fkp,fjp->fkj', exact, exact, precision=lax.Precision.HIGHEST)  5.85 us
  transfers between devices with their start and end apart: 1, of which 1 were waited for; matrix products, arithmetic and copies ran while one was open for 0% of the time, Pallas kernels for 0%

commit v1 on v0

--- a/solution.py
+++ b/solution.py
@@ -1,3 +1,4 @@
+import functools
 import jax
 import jax.numpy as jnp
 from jax import lax
@@ -8,8 +9,16 @@
 FOLDS = 8
 
 
+def pack_the_paths(load, peer_axis):
+    part_next = lax.all_gather(load, peer_axis)
+    return jnp.sum(part_next, 0)
+
+
+attach_copies_up = functools.partial(pack_the_paths, peer_axis=("lat", "lon"))
+
+
 def grid_total(partial_value):
-    return lax.psum(partial_value, ("lat", "lon"))
+    return attach_copies_up(partial_value)
 
 
 def on_device(samples, area_weight, ocean_count, omega):

time: 254 us -> 243 us (0.957)
  waiting for transfers between devices: 132 us -> 110 us
  other arithmetic: 87.7 us -> 93 us
  matrix products: 17.5 us -> 21.7 us
    psum x1, waiting for transfers between devices: 132 us -> 36.5 us  [on_device(): cross = lax.psum(partial_cross, ('lat', 'lon'))]
    all_gather x0 -> x1, waiting for transfers between devices: none -> 73.3 us  [pack_the_paths(): part_next = lax.all_gather(load, peer_axis)]
    reduce_sum x0 -> x1, other arithmetic: none -> 4.41 us  [pack_the_paths(): return jnp.sum(part_next, 0)]
    dot_general x1, matrix products: 3.7 us -> 6.7 us  [on_device(): jnp.einsum('sp,fkp->fsk', weighted.astype(jnp.float32), exact, precision=...]
  transfers between devices with their start and end apart: 1 -> 2, of which waited for: 1 -> 2; matrix products, arithmetic and copies ran while one was open for 0% -> 43% of each run, Pallas kernels for 0% -> 0%
where the time goes in v1:
time: 243 us; the launch traced here: 242 us
  waiting for transfers between devices  110 us (45%)
  other arithmetic  93 us (38%)
  matrix products  21.7 us (9%)
  between operations  14.8 us (6%)
  local copies, waits for them, and re-layouts  2.67 us (1%)
    all_gather x1, waiting for transfers between devices, pack_the_paths(): part_next = lax.all_gather(load, peer_axis)  73.3 us
    another operation x4, other arithmetic, on_device(): lower_factor = jnp.linalg.cholesky(gram)  47.8 us
    another operation x3, other arithmetic, on_device(): jax.scipy.linalg.solve_triangular(lower_factor, identity, lower=True)  40.1 us
    psum x1, waiting for transfers between devices, on_device(): cross = lax.psum(partial_cross, ('lat', 'lon'))  36.5 us
    dot_general x1, matrix products, on_device(): jnp.einsum('sp,fkp->fsk', weighted.astype(jnp.float32), exact, precision=...  6.7 us
    dot_general x1, matrix products, on_device(): jnp.einsum('fkp,fjp->fkj', exact, exact, precision=lax.Precision.HIGHEST)  6.2 us
  transfers between devices with their start and end apart: 2, of which 2 were waited for; matrix products, arithmetic and copies ran while one was open for 43% of the time, Pallas kernels for 0%

profile of v1, /device:TPU:0, one launch (start us, length us, event | category | flops | bytes accessed | tf_op | source)
XLA Modules:
  0.0 242.2 jit_solution(11312542352633324221)
XLA Ops:
  7.2 0.0 all-gather.3.cloned.1.call-start
  7.9 2.4 fusion.26
  10.3 0.0 copy-start
  10.3 2.5 %copy-done = f32[512,2816]{1,0:T(8,128)} copy-done((f32[512,2816]{1,0:T(8,128)}, f32[512,2816]{1,0:T(8,128)S(1)}, u32[]{:S(2)}) %copy-start) | copy-done | bytes 5767192
  12.8 0.0 copy-start.1
  12.8 6.2 %fusion.27 = f32[8,64,64]{2,1,0:T(8,128)} fusion(f32[8,64,2816]{2,1,0:T(8,128)S(1)} %bitcast.27), kind=kOutput, calls=%fused_computation.44 | convolution fusion | flops 1107296256 | bytes 5898240 | tf_op jit(solution)/shard_map/fkp,fjp->fkj/dot_general | solution.py:40
  19.0 0.0 all-gather.3.cloned.1.call-update
  19.0 0.2 all-reduce.2.cloned.1.call-start
  19.3 0.0 copy-done.1
  19.3 6.7 %fusion.2 = f32[8,256,64]{1,2,0:T(8,128)} fusion(f32[8,64,2816]{2,1,0:T(8,128)} %bitcast.28, bf16[256,2816]{1,0:T(8,128)(2,1)} %param.4, f32[2816]{0:T(1024)S(1)} %copy-done.1, pred[2816]{0:T(1024)(128)(4,1)S(1)} %iota_compare_fusion.2), kind=kOutput, calls=%fused_computation.4 | convolution fusion | flops 4432068608 | bytes 7747328 | tf_op jit(solution)/shard_map/sp,fkp->fsk/dot_general | solution.py:42
  26.0 0.0 all-reduce.2.cloned.1.call-update
  26.0 73.3 %all-gather.3.cloned.1.call-done = f32[256,64,64]{2,1,0:T(8,128)} async-done(((f32[8,64,64]{2,1,0:T(8,128)}), f32[256,64,64]{2,1,0:T(8,128)}) %all-gather.3.cloned.1.call-update) | async-done | bytes 4194320 | tf_op jit(solution)/shard_map/all_gather | solution.py:13
  99.3 4.4 %reduce_sum.9 = f32[8,64,64]{2,1,0:T(8,128)S(1)} reduce(f32[32,8,64,64]{3,2,1,0:T(8,128)} %bitcast.30, f32[]{:T(128)} %constant.79.clone.1), dimensions={0}, to_apply=%region_0.1 | reduce | flops 1015808 | bytes 4325380 | tf_op jit(solution)/shard_map/reduce_sum | solution.py:14
  103.7 0.1 copy.10
  103.9 0.7 fusion.8
  104.6 47.6 %custom-call.8 = f32[8,64,64]{2,1,0:T(8,128)S(1)} custom-call(f32[8,64,64]{2,1,0:T(8,128)} %fusion.8), custom_call_target="Cholesky" | custom-call | tf_op jit(solution)/shard_map/jit(cholesky)/cholesky | solution.py:45
  152.3 0.1 compare_reduce_fusion
  152.4 0.1 select_bitcast_fusion
  152.5 40.0 %custom-call.9 = f32[8,1,64,64]{2,3,1,0:T(8,128)} custom-call(f32[8,1,64,64]{3,2,1,0:T(8,128)S(1)} %select_bitcast_fusion), custom_call_target="InvertDiagBlocksLowerTriangular" | custom-call | tf_op jit(solution)/shard_map/jit(_solve_triangular)/vmap()/triangular_solve | solution.py:47
  192.5 1.5 fusion.6
  194.0 2.5 %convolution_convert_fusion = bf16[8,64,2816]{2,1,0:T(8,128)(2,1)} fusion(bf16[8,64,2816]{2,1,0:T(8,128)(2,1)S(1)} %bitcast.29, f32[8,64,64]{2,1,0:T(8,128)S(1)} %fusion.6), kind=kOutput, calls=%fused_computation | convolution fusion | flops 186056704 | bytes 5898240 | tf_op jit(solution)/shard_map/fkj,fjp->fkp/dot_general | solution.py:49
  196.5 36.5 %all-reduce.2.cloned.1.call-done = f32[8,256,64]{1,2,0:T(8,128)} async-done(((f32[8,256,64]{1,2,0:T(8,128)}), f32[8,256,64]{1,2,0:T(8,128)}) %all-reduce.2.cloned.1.call-update) | async-done | bytes 524304 | tf_op jit(solution)/shard_map/psum | solution.py:54
  233.0 2.4 %fusion.9 = f32[8,256,64]{1,2,0:T(8,128)} fusion(f32[8,256,64]{1,2,0:T(8,128)} %all-reduce.2.cloned.1.call-done, f32[8,64,64]{2,1,0:T(8,128)S(1)} %fusion.6), kind=kOutput, calls=%fused_computation.11 | convolution fusion | flops 100696064 | bytes 1179648 | tf_op jit(solution)/shard_map/fsj,fkj->fsk/dot_general | solution.py:55
  (7 shorter events, 0.1 us)
Async XLA Ops:
  7.2 92.1 %all-gather.3.cloned.1.call-start = ((), (), s32[]{:S(2)}) async-start(), calls=%async_computation.1 | async-start | bytes 8650752 | tf_op jit(solution)/shard_map/all_gather | solution.py:13
  10.3 2.5 %copy-start = (f32[512,2816]{1,0:T(8,128)}, f32[512,2816]{1,0:T(8,128)S(1)}, u32[]{:S(2)}) copy-start(f32[512,2816]{1,0:T(8,128)S(1)} %get-tuple-element.3) | copy-start | bytes 17301508
  12.8 6.5 %copy-start.1 = (f32[2816]{0:T(1024)S(1)}, f32[2816]{0:T(1024)}, u32[]{:S(2)}) copy-start(f32[2816]{0:T(1024)} %param.5) | copy-start | bytes 33796
  19.0 213.9 %all-reduce.2.cloned.1.call-start = ((), (), s32[]{:S(2)}) async-start(), calls=%async_computation | async-start | bytes 1048576 | tf_op jit(solution)/shard_map/psum | solution.py:54
Sparse Core Ops, SparseCore 0:
  19.2 80.1 all-gather.2
  105.2 127.7 all-reduce.1
